TPU v7x, 128 devices: a whole 4x4x4 slice. The times are simulated.
128 devices in a mesh: outer: 4 (over z_lo, core), inner: 32 (over z_hi, y, x).
Axes of the slice: x: 4, y: 4, z: 4 (z_hi: 2, z_lo: 2; z = z_hi * 2 + z_lo), core: 2. Of those that a mesh axis runs over, the one named last changes fastest.
Arguments:
- inputs: bfloat16 [131072, 1024], P(('outer', 'inner')), may hold values from -24 to 24
- queries: bfloat16 [131072, 1024], P(('outer', 'inner')), may hold values from -6 to 6
- keys: bfloat16 [131072, 1024], P(('outer', 'inner')), may hold values from -6 to 6
- values: bfloat16 [131072, 1024], P(('outer', 'inner')), may hold values from -6 to 6
- out_grad: bfloat16 [131072, 1024], P(('outer', 'inner')), may hold values from -6 to 6
- master: float32 [1024, 1024], P('inner'), may hold values from -0.1875 to 0.1875
- moment1: float32 [1024, 1024], P('inner'), may hold values from -6 to 6
- moment2: float32 [1024, 1024], P('inner'), may hold values from 0.05 to 2
Outputs:
- query_grad: bfloat16 [131072, 1024], P(('outer', 'inner'))
- key_grad: bfloat16 [131072, 1024], P(('outer', 'inner'))
- new_master: float32 [1024, 1024], P('inner')
- new_moment1: float32 [1024, 1024], P('inner')
- new_moment2: float32 [1024, 1024], P('inner')
- weights: bfloat16 [1024, 1024], replicated
All inputs are finite; a program needn't handle non-finite values.
Results may differ from a plain program's by a relative error of at most 0.008.
Values may be sent and summed in bfloat16 or wider, within the bound.
A program may use at most 192 MiB of HBM per device.

v0:
```python
import math
import jax
import jax.numpy as jnp
from jax import lax
from jax.sharding import PartitionSpec as P

H = 8
HD = 128
BLK = 512


def entering(array, axis, combine, identity, reverse):
    count, place = (lax.axis_size(axis), lax.axis_index(axis))
    everything = lax.all_gather(array, axis)
    start = jnp.broadcast_to(jnp.asarray(identity, array.dtype), array.shape)

    def turn(k, before):
        at = count - 1 - k if reverse else k
        reached = at > place if reverse else at < place
        new = combine(before, everything[at])
        return jnp.where(reached, new, before)

    return lax.fori_loop(0, count, turn, start)


def add_states(earlier, later):
    return earlier + later


def split_state(state):
    upper = state.astype(jnp.bfloat16)
    lower = (state - upper.astype(jnp.float32)).astype(jnp.bfloat16)
    return (upper, lower)


def state_times_query(form, rows, state):
    upper, lower = split_state(state)
    first = jnp.einsum(form, rows, upper, preferred_element_type=jnp.float32)
    return first + jnp.einsum(form, rows, lower, preferred_element_type=jnp.float32)


def local(inputs, queries, keys, values, out_grad, master, moment1, moment2):
    rows_here = inputs.shape[0]
    width = inputs.shape[1]
    n_outer = lax.axis_size("outer")
    n_inner = lax.axis_size("inner")
    total_tokens = rows_here * n_outer * n_inner
    att_scale = 1.0 / math.sqrt(HD * total_tokens)
    grad_scale = 1.0 / math.sqrt(total_tokens)
    blocks = rows_here // BLK
    shape_four = (blocks, BLK, H, HD)
    query_blocks = queries.reshape(shape_four)
    key_blocks = keys.reshape(shape_four)
    value_blocks = values.reshape(shape_four)
    grad_blocks = out_grad.reshape(shape_four)
    kv_block = jnp.einsum(
        "nthk,nthv->nhkv", key_blocks, value_blocks, preferred_element_type=jnp.float32
    )
    qg_block = jnp.einsum(
        "nthv,nthk->nhvk", grad_blocks, query_blocks, preferred_element_type=jnp.float32
    )
    own_kv = jnp.sum(kv_block, 0)
    own_qg = jnp.sum(qg_block, 0)
    zero_state = jnp.zeros_like(own_kv)
    kv_earlier = entering(own_kv, ("outer", "inner"), add_states, zero_state, False)
    qg_later = entering(own_qg, ("outer", "inner"), add_states, zero_state, True)
    key_value_prior = kv_earlier[None] + jnp.concatenate(
        [zero_state[None], jnp.cumsum(kv_block, 0)[:-1]], 0
    )
    qg_reverse = jnp.cumsum(qg_block[::-1], 0)[::-1]
    qg_after = qg_later[None] + jnp.concatenate([qg_reverse[1:], zero_state[None]], 0)
    causal = jnp.arange(BLK)[:, None] >= jnp.arange(BLK)[None, :]
    query_parts = []
    key_parts = []
    for block_number in range(blocks):
        query_b = query_blocks[block_number]
        key_block_rows = key_blocks[block_number]
        value_block_rows = value_blocks[block_number]
        block_gradient = grad_blocks[block_number]
        scores = jnp.einsum(
            "thv,shv->hts", block_gradient, value_block_rows, preferred_element_type=jnp.float32
        )
        scores = jnp.where(causal[None], scores, 0.0).astype(jnp.bfloat16)
        query_gradient = jnp.einsum(
            "hts,shk->thk", scores, key_block_rows, preferred_element_type=jnp.float32
        )
        query_gradient = query_gradient + state_times_query(
            "rgn,gfn->rgf", block_gradient, key_value_prior[block_number]
        )
        dkey = jnp.einsum("hts,thk->shk", scores, query_b, preferred_element_type=jnp.float32)
        dkey = dkey + state_times_query("shv,hvk->shk", value_block_rows, qg_after[block_number])
        query_parts.append((query_gradient * att_scale).astype(jnp.bfloat16).reshape(BLK, width))
        key_parts.append((dkey * att_scale).astype(jnp.bfloat16).reshape(BLK, width))
    query_grad = jnp.concatenate(query_parts, 0)
    key_grad = jnp.concatenate(key_parts, 0)
    product = lax.dot_general(
        inputs, key_grad, (((0,), (0,)), ((), ())), preferred_element_type=jnp.float32
    )
    shares = lax.psum_scatter(product * grad_scale, "inner", scatter_dimension=0, tiled=True)
    grad = lax.psum(shares, "outer")
    new_moment1 = 0.9 * moment1 + 0.1 * grad
    new_moment2 = 0.95 * moment2 + 0.05 * grad * grad
    new_master = master - 0.01 * (new_moment1 / (jnp.sqrt(new_moment2) + 1e-08) + 0.1 * master)
    weights = lax.all_gather(new_master.astype(jnp.bfloat16), "inner", axis=0, tiled=True)
    return (query_grad, key_grad, new_master, new_moment1, new_moment2, weights)


def solution(mesh):
    in_specs = (
        P(("outer", "inner"), None),
        P(("outer", "inner"), None),
        P(("outer", "inner"), None),
        P(("outer", "inner"), None),
        P(("outer", "inner"), None),
        P("inner", None),
        P("inner", None),
        P("inner", None),
    )
    out_specs = (
        P(("outer", "inner"), None),
        P(("outer", "inner"), None),
        P("inner", None),
        P("inner", None),
        P("inner", None),
        P(),
    )
    return jax.shard_map(local, mesh=mesh, in_specs=in_specs, out_specs=out_specs, check_vma=False)
```

profile of v0, /device:TPU:1, one launch (start us, length us, event | category | flops | bytes accessed | tf_op | source)
XLA Modules:
  0.0 1391.0 jit_solution(7960946358874442010)
XLA Ops:
  7.2 2.4 copy.175
  10.2 2.9 fusion.43
  13.3 2.3 rev.4
  15.6 3.0 fusion.38
  18.6 2.3 copy.136
  20.9 2.3 copy.143
  23.2 3.0 fusion.40
  26.2 2.3 copy.170
  28.5 2.3 copy.172
  30.8 3.1 fusion.41
  33.8 2.3 copy.169
  36.1 2.3 copy.171
  38.5 5.1 select_convert_fusion
  43.6 3.4 select_convert_fusion.1
  47.0 353.1 %all-gather.10.cloned.1.call-done = f32[1024,128,128]{2,1,0:T(8,128)} async-done(((f32[8,128,128]{2,1,0:T(8,128)}), f32[1024,128,128]{2,1,0:T(8,128)}) %all-gather.10.cloned.1.call-update) | async-done | bytes 67108880 | tf_op jit(solution)/shard_map/all_gather | solution.py:14
  400.2 160.7 %while.31 = (s32[]{:T(128)}, f32[8,128,128]{2,1,0:T(8,128)S(1)}, s32[]{:T(128)}, f32[128,8,128,128]{3,2,1,0:T(8,128)}, s32[]{:T(128)}, /*index=5*/s32[]{:T(128)}, s32[]{:T(128)}, s32[]{:T(128)}) while((s32[]{:T(128)}, f32[8,128,128]{2,1,0:T(8,128)S(1)}, s32[]{:T(128)}, f32[128,8,128,128]{3,2,1,0:T(8,128)}, s32[]{:T(128)}, ...), condition=%wide.region_6.7_spmd.clone, body=%wide.region_5.6_spmd.clone.sunk | while | flops 393224 | bytes 1573027 | solution.py:23
  400.2 1.2 add_select_fusion.5
  560.9 1.5 fusion.14
  564.2 1.8 fusion.21
  566.0 1.8 fusion.28
  567.8 1.7 fusion.1
  569.5 2.4 copy.149
  571.9 5.2 fusion.3
  577.1 2.4 copy.148
  579.4 1.4 pad_maximum_fusion.1
  580.8 1.3 copy-done.19
  582.2 4.5 multiply_bitcast_fusion
  586.6 5.3 copy.167
  592.2 1.3 copy-done.12
  593.5 2.0 copy.174
  595.5 1.9 copy.173
  597.4 166.0 %reduce-scatter.4.cloned.1.call-done = f32[32,1024]{1,0:T(8,128)} async-done(((f32[1024,1024]{1,0:T(8,128)}), f32[32,1024]{1,0:T(8,128)}) %reduce-scatter.4.cloned.1.call-update) | async-done | bytes 131088 | tf_op jit(solution)/shard_map/reduce_scatter | solution.py:99
  763.5 3.5 fusion.42
  767.8 1.7 fusion.39
  769.5 1.3 copy.122
  771.4 48.4 %all-reduce.3.cloned.1.call-done = f32[32,1024]{1,0:T(8,128)} async-done(((f32[32,1024]{1,0:T(8,128)}), f32[32,1024]{1,0:T(8,128)}) %all-reduce.3.cloned.1.call-update) | async-done | bytes 131088 | tf_op jit(solution)/shard_map/psum | solution.py:100
  819.8 1.7 fusion.36
  821.5 384.5 %all-gather.8.cloned.1.call-done = f32[1024,128,128]{2,1,0:T(8,128)} async-done(((f32[8,128,128]{2,1,0:T(8,128)}), f32[1024,128,128]{2,1,0:T(8,128)}) %all-gather.8.cloned.1.call-update) | async-done | bytes 67108880 | tf_op jit(solution)/shard_map/all_gather | solution.py:14
  1206.0 160.2 %while.30 = (s32[]{:T(128)}, f32[8,128,128]{2,1,0:T(8,128)S(1)}, s32[]{:T(128)}, f32[128,8,128,128]{3,2,1,0:T(8,128)}, s32[]{:T(128)}, /*index=5*/s32[]{:T(128)}) while((s32[]{:T(128)}, f32[8,128,128]{2,1,0:T(8,128)S(1)}, s32[]{:T(128)}, f32[128,8,128,128]{3,2,1,0:T(8,128)}, s32[]{:T(128)}, /*index=5*/s32[]{:T(128)}) %tuple.83), condition=%wide.region_2.3_spmd.clone, body=%wide.region_1.0_spmd.clone.sunk | while | flops 393220 | bytes 1572965 | solution.py:23
  1259.8 1.2 add_select_fusion.4
  1273.6 1.2 add_select_fusion.4
  1368.2 1.3 copy-done.4
  1369.6 2.5 fusion.5
  1372.1 2.4 copy.135
  1375.3 1.3 copy-done.2
  1377.0 1.5 fusion.7
  1379.7 1.5 pad_maximum_fusion
  1381.2 3.2 copy.207
  (325 shorter events, 319.1 us)
Async XLA Ops:
  7.2 575.0 %copy-start = (bf16[1024,1024]{1,0:T(8,128)(2,1)S(1)}, bf16[1024,1024]{1,0:T(8,128)(2,1)}, u32[]{:S(2)}) copy-start(bf16[1024,1024]{1,0:T(8,128)(2,1)} %param.12) | copy-start | bytes 6291460
  7.2 393.0 %all-gather.10.cloned.1.call-start = ((), (), s32[]{:S(2)}) async-start(), calls=%async_computation.4 | async-start | bytes 67633152 | tf_op jit(solution)/shard_map/all_gather | solution.py:14
  7.2 2.4 copy-start.11
  13.2 750.2 %reduce-scatter.4.cloned.1.call-start = ((), (), s32[]{:S(2)}) async-start(), calls=%async_computation.5 | async-start | bytes 4325376 | tf_op jit(solution)/shard_map/reduce_scatter | solution.py:99
  38.5 5.1 copy-start.5
  38.5 5.1 copy-start.8
  400.2 160.7 %copy-start.24 = (pred[2]{0:T(512)(128)(4,1)S(1)}, pred[2]{0:T(512)(128)(4,1)}, u32[]{:S(2)}) copy-start(pred[2]{0:T(512)(128)(4,1)} %constant.95.clone.1) | copy-start | bytes 10
  560.9 1.5 copy-start.10
  562.9 1.2 copy-start.9
  564.2 3.6 copy-start.3
  566.0 1.8 copy-start.15
  569.5 2.4 copy-start.14
  577.1 2.4 copy-start.18
  580.8 1.3 copy-start.19
  591.9 1.6 copy-start.12
  592.0 227.8 %all-reduce.3.cloned.1.call-start = ((), (), s32[]{:S(2)}) async-start(), calls=%async_computation.1 | async-start | bytes 262144 | tf_op jit(solution)/shard_map/psum | solution.py:100
  593.5 2.0 copy-start.13
  595.5 168.0 %copy-start.20 = (bf16[128,8,8,128]{3,2,1,0:T(8,128)(2,1)S(1)}, bf16[128,8,8,128]{3,2,1,0:T(8,128)(2,1)}, u32[]{:S(2)}) copy-start(bf16[128,8,8,128]{3,2,1,0:T(8,128)(2,1)} %copy.174) | copy-start | bytes 6291460
  763.4 442.5 %all-gather.8.cloned.1.call-start = ((), (), s32[]{:S(2)}) async-start(), calls=%async_computation.3 | async-start | bytes 67633152 | tf_op jit(solution)/shard_map/all_gather | solution.py:14
  767.1 614.1 %all-gather.6.cloned.1.call-start = ((), (), s32[]{:S(2)}) async-start(), calls=%async_computation.2 | async-start | bytes 2162688 | tf_op jit(solution)/shard_map/all_gather | solution.py:104
  769.5 50.3 %copy-start.21 = (f32[32,1024]{1,0:T(8,128)S(1)}, f32[32,1024]{1,0:T(8,128)}, u32[]{:S(2)}) copy-start(f32[32,1024]{1,0:T(8,128)} %param.17) | copy-start | bytes 393220
  769.5 50.3 %copy-start.22 = (f32[32,1024]{1,0:T(8,128)S(1)}, f32[32,1024]{1,0:T(8,128)}, u32[]{:S(2)}) copy-start(f32[32,1024]{1,0:T(8,128)} %param.19) | copy-start | bytes 393220
  769.5 50.3 %copy-start.23 = (f32[32,1024]{1,0:T(8,128)S(1)}, f32[32,1024]{1,0:T(8,128)}, u32[]{:S(2)}) copy-start(f32[32,1024]{1,0:T(8,128)} %param.18) | copy-start | bytes 393220
  1366.2 1.2 copy-start.7
  1367.4 2.2 copy-start.4
  1372.1 2.4 copy-start.6
  1374.4 2.2 copy-start.2
  1374.8 2.2 copy-start.16
  1378.5 1.2 copy-start.17
  1381.2 3.2 copy-start.1
Sparse Core Ops, SparseCore 0:
  13.3 386.7 all-gather.9
  592.1 171.2 reduce-scatter.3
  765.9 53.8 all-reduce.2
  821.9 384.0 all-gather.7
  1208.9 70.3 all-gather.5
where the time goes:
time: 1400 us; the launch traced here: 1390 us
  waiting for transfers between devices  952 us (68%)
  other arithmetic  321 us (23%)
  local copies, waits for them, and re-layouts  60.2 us (4%)
  matrix products  36.5 us (3%)
  between operations  14.1 us (1%)
    all_gather x2, waiting for transfers between devices, entering(): everything = lax.all_gather(array, axis)  738 us
    select_n x256, other arithmetic, turn(): return jnp.where(reached, new, before)  314 us
    reduce_scatter x1, waiting for transfers between devices, local(): lax.psum_scatter(product * grad_scale, 'inner', scatter_dimension=0, tile...  166 us
    psum x1, waiting for transfers between devices, local(): grad = lax.psum(shares, 'outer')  48.4 us
    unnamed x60, local copies, waits for them, and re-layouts  33 us
  transfers between devices with their start and end apart: 5, of which 4 were waited for; matrix products, arithmetic and copies ran while one was open for 15% of the time, Pallas kernels for 0%

commit v1 on v0

--- a/solution.py
+++ b/solution.py
@@ -97,7 +97,7 @@
         inputs, key_grad, (((0,), (0,)), ((), ())), preferred_element_type=jnp.float32
     )
     shares = lax.psum_scatter(product * grad_scale, "inner", scatter_dimension=0, tiled=True)
-    grad = lax.psum(shares, "outer")
+    grad = jnp.sum(lax.all_gather(shares, "outer"), axis=0)
     new_moment1 = 0.9 * moment1 + 0.1 * grad
     new_moment2 = 0.95 * moment2 + 0.05 * grad * grad
     new_master = master - 0.01 * (new_moment1 / (jnp.sqrt(new_moment2) + 1e-08) + 0.1 * master)

time: 1400 us -> 1360 us (0.971)
  waiting for transfers between devices: 952 us -> 887 us
  blocking collectives: 0 us -> 30.1 us
    psum x1 -> x0, waiting for transfers between devices: 48.4 us -> none  [local(): grad = lax.psum(shares, 'outer')]
    all_gather x0 -> x1, blocking collectives: none -> 30.1 us  [local(): grad = jnp.sum(lax.all_gather(shares, 'outer'), axis=0)]
    unnamed x60 -> x58, local copies, waits for them, and re-layouts: 33 us -> 31.4 us
  transfers between devices with their start and end apart: 5 -> 4, of which waited for: 4 -> 3; matrix products, arithmetic and copies ran while one was open for 15% -> 15% of each run, Pallas kernels for 0% -> 0%
where the time goes in v1:
time: 1360 us; the launch traced here: 1350 us
  waiting for transfers between devices  887 us (65%)
  other arithmetic  320 us (24%)
  local copies, waits for them, and re-layouts  58.6 us (4%)
  matrix products  34.9 us (3%)
  blocking collectives  30.1 us (2%)
  between operations  14.1 us (1%)
    all_gather x2, waiting for transfers between devices, entering(): everything = lax.all_gather(array, axis)  725 us
    select_n x256, other arithmetic, turn(): return jnp.where(reached, new, before)  314 us
    reduce_scatter x1, waiting for transfers between devices, local(): lax.psum_scatter(product * grad_scale, 'inner', scatter_dimension=0, tile...  161 us
    unnamed x58, local copies, waits for them, and re-layouts  31.4 us
    all_gather x1, blocking collectives, local(): grad = jnp.sum(lax.all_gather(shares, 'outer'), axis=0)  30.1 us
  transfers between devices with their start and end apart: 4, of which 3 were waited for; matrix products, arithmetic and copies ran while one was open for 15% of the time, Pallas kernels for 0%

profile of v1, /device:TPU:1, one launch (start us, length us, event | category | flops | bytes accessed | tf_op | source)
XLA Modules:
  0.0 1351.9 jit_solution(8574302875787390313)
XLA Ops:
  7.2 2.4 copy.120
  10.2 2.9 fusion.43
  13.3 2.3 rev.4
  15.6 3.0 fusion.38
  18.7 2.3 copy.81
  20.9 2.3 copy.88
  23.2 3.0 fusion.40
  26.2 2.3 copy.115
  28.6 2.3 copy.117
  30.9 3.1 fusion.41
  33.9 2.3 copy.114
  36.3 2.3 copy.116
  38.7 5.1 select_convert_fusion
  43.7 3.4 select_convert_fusion.1
  47.1 353.0 %all-gather.11.cloned.1.call-done = f32[1024,128,128]{2,1,0:T(8,128)} async-done(((f32[8,128,128]{2,1,0:T(8,128)}), f32[1024,128,128]{2,1,0:T(8,128)}) %all-gather.11.cloned.1.call-update) | async-done | bytes 67108880 | tf_op jit(solution)/shard_map/all_gather | solution.py:14
  400.2 160.7 %while.31 = (s32[]{:T(128)}, f32[8,128,128]{2,1,0:T(8,128)S(1)}, s32[]{:T(128)}, f32[128,8,128,128]{3,2,1,0:T(8,128)}, s32[]{:T(128)}, /*index=5*/s32[]{:T(128)}, s32[]{:T(128)}, s32[]{:T(128)}) while((s32[]{:T(128)}, f32[8,128,128]{2,1,0:T(8,128)S(1)}, s32[]{:T(128)}, f32[128,8,128,128]{3,2,1,0:T(8,128)}, s32[]{:T(128)}, ...), condition=%wide.region_6.7_spmd.clone, body=%wide.region_5.6_spmd.clone.sunk | while | flops 393224 | bytes 1573027 | solution.py:23
  400.2 1.2 add_select_fusion.5
  560.9 1.5 fusion.14
  564.2 1.8 fusion.21
  566.0 1.8 fusion.28
  567.8 1.8 fusion.1
  569.6 2.4 copy.94
  571.9 5.2 fusion.3
  577.2 2.4 copy.93
  579.5 1.4 pad_maximum_fusion.1
  580.9 1.3 copy-done.19
  582.2 4.4 multiply_bitcast_fusion
  586.6 5.4 copy.112
  592.3 1.3 copy-done.12
  595.8 1.9 fusion.42
  598.4 1.7 fusion.39
  600.2 1.3 copy.67
  602.1 161.5 %reduce-scatter.4.cloned.1.call-done = f32[32,1024]{1,0:T(8,128)} async-done(((f32[1024,1024]{1,0:T(8,128)}), f32[32,1024]{1,0:T(8,128)}) %reduce-scatter.4.cloned.1.call-update) | async-done | bytes 131088 | tf_op jit(solution)/shard_map/reduce_scatter | solution.py:99
  763.5 30.1 %all-gather.2 = f32[128,1024]{1,0:T(8,128)S(1)} all-gather(f32[32,1024]{1,0:T(8,128)} %reduce-scatter.4.cloned.1.call-done), channel_id=4, replica_groups=mesh['outer'=4,'inner'=32] {'outer'}, dimensions={0}, use_global_device_ids=true | all-gather | bytes 655360 | tf_op jit(solution)/shard_map/all_gather | solution.py:100
  794.5 372.5 %all-gather.9.cloned.1.call-done = f32[1024,128,128]{2,1,0:T(8,128)} async-done(((f32[8,128,128]{2,1,0:T(8,128)}), f32[1024,128,128]{2,1,0:T(8,128)}) %all-gather.9.cloned.1.call-update) | async-done | bytes 67108880 | tf_op jit(solution)/shard_map/all_gather | solution.py:14
  1166.9 160.2 %while.30 = (s32[]{:T(128)}, f32[8,128,128]{2,1,0:T(8,128)S(1)}, s32[]{:T(128)}, f32[128,8,128,128]{3,2,1,0:T(8,128)}, s32[]{:T(128)}, /*index=5*/s32[]{:T(128)}) while((s32[]{:T(128)}, f32[8,128,128]{2,1,0:T(8,128)S(1)}, s32[]{:T(128)}, f32[128,8,128,128]{3,2,1,0:T(8,128)}, s32[]{:T(128)}, /*index=5*/s32[]{:T(128)}) %tuple.80), condition=%wide.region_2.3_spmd.clone, body=%wide.region_1.0_spmd.clone.sunk | while | flops 393220 | bytes 1572965 | solution.py:23
  1179.4 1.2 add_select_fusion.4
  1180.7 1.2 add_select_fusion.4
  1209.5 1.2 add_select_fusion.4
  1220.8 1.2 add_select_fusion.4
  1234.5 1.2 add_select_fusion.4
  1329.2 1.3 copy-done.4
  1330.5 2.5 fusion.5
  1333.0 2.4 copy.80
  1336.2 1.3 copy-done.2
  1338.0 1.5 fusion.7
  1340.7 1.5 pad_maximum_fusion
  1342.2 3.2 copy.151
  (322 shorter events, 318.3 us)
Async XLA Ops:
  7.2 575.1 %copy-start = (bf16[1024,1024]{1,0:T(8,128)(2,1)S(1)}, bf16[1024,1024]{1,0:T(8,128)(2,1)}, u32[]{:S(2)}) copy-start(bf16[1024,1024]{1,0:T(8,128)(2,1)} %param.12) | copy-start | bytes 6291460
  7.2 393.0 %all-gather.11.cloned.1.call-start = ((), (), s32[]{:S(2)}) async-start(), calls=%async_computation.3 | async-start | bytes 67633152 | tf_op jit(solution)/shard_map/all_gather | solution.py:14
  7.2 2.4 copy-start.11
  13.2 750.3 %reduce-scatter.4.cloned.1.call-start = ((), (), s32[]{:S(2)}) async-start(), calls=%async_computation.4 | async-start | bytes 4325376 | tf_op jit(solution)/shard_map/reduce_scatter | solution.py:99
  38.6 5.1 copy-start.5
  38.6 5.1 copy-start.8
  400.2 160.7 %copy-start.23 = (pred[2]{0:T(512)(128)(4,1)S(1)}, pred[2]{0:T(512)(128)(4,1)}, u32[]{:S(2)}) copy-start(pred[2]{0:T(512)(128)(4,1)} %constant.95.clone.1) | copy-start | bytes 10
  560.9 1.5 copy-start.10
  562.9 1.2 copy-start.9
  564.1 3.6 copy-start.3
  566.0 1.8 copy-start.15
  569.6 2.4 copy-start.14
  577.2 2.4 copy-start.18
  580.9 1.3 copy-start.19
  592.0 1.6 copy-start.12
  592.0 574.9 %all-gather.9.cloned.1.call-start = ((), (), s32[]{:S(2)}) async-start(), calls=%async_computation.2 | async-start | bytes 67633152 | tf_op jit(solution)/shard_map/all_gather | solution.py:14
  593.6 1.6 copy-start.13
  597.7 744.4 %all-gather.7.cloned.1.call-start = ((), (), s32[]{:S(2)}) async-start(), calls=%async_computation.1 | async-start | bytes 2162688 | tf_op jit(solution)/shard_map/all_gather | solution.py:104
  601.5 192.1 %copy-start.20 = (f32[32,1024]{1,0:T(8,128)S(1)}, f32[32,1024]{1,0:T(8,128)}, u32[]{:S(2)}) copy-start(f32[32,1024]{1,0:T(8,128)} %param.17) | copy-start | bytes 393220
  601.5 192.1 %copy-start.21 = (f32[32,1024]{1,0:T(8,128)S(1)}, f32[32,1024]{1,0:T(8,128)}, u32[]{:S(2)}) copy-start(f32[32,1024]{1,0:T(8,128)} %param.19) | copy-start | bytes 393220
  601.5 192.1 %copy-start.22 = (f32[32,1024]{1,0:T(8,128)S(1)}, f32[32,1024]{1,0:T(8,128)}, u32[]{:S(2)}) copy-start(f32[32,1024]{1,0:T(8,128)} %param.18) | copy-start | bytes 393220
  1327.1 1.2 copy-start.7
  1328.4 2.2 copy-start.4
  1333.0 2.4 copy-start.6
  1335.4 2.2 copy-start.2
  1335.8 2.2 copy-start.16
  1339.5 1.2 copy-start.17
  1342.2 3.2 copy-start.1
Sparse Core Ops, SparseCore 0:
  13.3 386.7 all-gather.10
  592.1 171.3 reduce-scatter.3
  765.8 401.1 all-gather.8
  1169.9 70.3 all-gather.6
